TPU v7x, 256 devices: a whole 4x4x8 slice. The times are simulated.
256 devices in a mesh: freq: 4 (over y), mx: 8 (over x, core), my: 8 (over z).
Axes of the slice: x: 4, y: 4, z: 8, core: 2. Of those that a mesh axis runs over, the one named last changes fastest.
Arguments:
- adjoint_rhs: float32 [4, 2, 3, 512, 2048], P('freq', None, None, 'mx', 'my'), may hold values from -4 to 6
- state: bfloat16 [4, 2, 3, 512, 2048], P('freq', None, None, 'mx', 'my'), may hold values from -1.5 to 1.5
- density: float32 [512, 2048], P('mx', 'my'), may hold values from 0.85 to 1
- stiffness: float32 [512, 2048], P('mx', 'my'), may hold values from 1.5 to 4
- mass: float32 [512, 2048], P('mx', 'my'), may hold values from 0.2 to 1
- omega: float32 [4], P('freq'), may hold values from 0.15 to 0.45
- send_rows: int32 [64, 2048], P(('mx', 'my')), may hold values from 0 to 16383, as said below
- recv_rows: int32 [64, 2048], P(('mx', 'my')), may hold values from 0 to 16383, as said below
- mortar_weight: float32 [64, 2048], P(('mx', 'my')), may hold values from 0 to 1.5, as said below
Outputs:
- adjoint: float32 [4, 2, 3, 512, 2048], P('freq', None, None, 'mx', 'my')
- filtered_sensitivity: float32 [512, 2048], P('mx', 'my')
Inputs may be any that keep to these rules, and one draw needn't show every extreme that they name: `send_rows`: a local cell of the sending device; slots past the live count of a device pair hold 0. `recv_rows`: a local cell of the receiving device; empty slots hold 0. Live slots of a pair come first, up to 32 of them. `mortar_weight`: zero exactly in empty slots, at least 0.5 in live ones; every receiving device has a source device with all 32 slots live.
All inputs are finite; a program needn't handle non-finite values.
Results may differ from a plain program's by a relative error of at most 0.0003.
Values may be sent and summed in bfloat16 or wider, within the bound.
A program may use at most 64 MiB of HBM per device.

v0:
```python
import jax
import jax.numpy as jnp
from jax import lax
from jax.sharding import PartitionSpec as P

ITERS = 20


def extended(x, sides, width):
    for axis, dim in sides:
        size, length = (lax.axis_size(axis), x.shape[dim])
        up = [(i, (i + 1) % size) for i in range(size - 1)]
        down = [(j, i) for i, j in up]
        last = lax.slice_in_dim(x, length - width, length, axis=dim)
        first = lax.slice_in_dim(x, 0, width, axis=dim)
        before = lax.ppermute(last, axis, up)
        after = lax.ppermute(first, axis, down)
        x = jnp.concatenate([before, x, after], axis=dim)
    return x


def on_device(
    adjoint_rhs, state, density, stiffness, mass, omega, send_rows, recv_rows, mortar_weight
):
    rows_x, rows_y = density.shape
    cells = rows_x * rows_y
    w = omega[0]
    stiff = density**3 * stiffness
    dstiff = 3.0 * density**2 * stiffness
    rmass = density * mass
    sources = send_rows[0]
    targets = recv_rows[0]
    weights = mortar_weight[0]
    mdiag = jnp.zeros((cells,), jnp.float32).at[targets].add(weights).reshape(rows_x, rows_y)
    real_d = 4.4 * stiff + 0.3 + mdiag - w * w * rmass
    imag_d = 0.2 * w * (stiff + rmass)
    den = real_d * real_d + imag_d * imag_d
    rhs = adjoint_rhs.reshape(6, rows_x, rows_y)

    def mortar(field):
        sent = field.reshape(6, cells)[:, sources]
        got = lax.all_to_all(sent, ("mx", "my"), split_axis=1, concat_axis=1, tiled=True)
        added = jnp.zeros((6, cells), jnp.float32).at[:, targets].add(got * weights)
        return added.reshape(6, rows_x, rows_y)

    def sweep(step, field):
        padded = extended(field, (("mx", 1), ("my", 2)), 1)
        beside = (
            padded[:, 2:, 1:-1] + padded[:, :-2, 1:-1] + padded[:, 1:-1, 2:] + padded[:, 1:-1, :-2]
        )
        h = rhs + stiff * beside + mortar(field)
        new_re = (h[:3] * real_d + h[3:] * imag_d) / den
        new_im = (h[3:] * real_d - h[:3] * imag_d) / den
        return jnp.concatenate([new_re, new_im], axis=0)

    field = lax.fori_loop(0, ITERS, sweep, jnp.zeros((6, rows_x, rows_y), jnp.float32))
    state_six = state.reshape(6, rows_x, rows_y)
    state_pad = extended(state_six, (("mx", 1), ("my", 2)), 1).astype(jnp.float32)
    u = state_six.astype(jnp.float32)
    nb = (
        state_pad[:, 2:, 1:-1]
        + state_pad[:, :-2, 1:-1]
        + state_pad[:, 1:-1, 2:]
        + state_pad[:, 1:-1, :-2]
    )
    da = 4.4 * dstiff - w * w * mass
    db = 0.2 * w * (dstiff + mass)
    t_re = da * u[:3] - db * u[3:] - dstiff * nb[:3]
    t_im = da * u[3:] + db * u[:3] - dstiff * nb[3:]
    sens = -jnp.sum(field[:3] * t_re - field[3:] * t_im, axis=0)
    total = lax.psum(sens, "freq")
    weighted = extended(density * total, (("mx", 0), ("my", 1)), 1)
    filt = weighted[1:-1, 1:-1]
    filt = filt + 0.5 * (
        weighted[2:, 1:-1] + weighted[:-2, 1:-1] + weighted[1:-1, 2:] + weighted[1:-1, :-2]
    )
    filt = filt + 0.25 * (
        weighted[2:, 2:] + weighted[:-2, :-2] + weighted[2:, :-2] + weighted[:-2, 2:]
    )
    return (field.reshape(1, 2, 3, rows_x, rows_y), filt / (4.0 * density))


def solution(mesh):
    return jax.shard_map(
        on_device,
        mesh=mesh,
        in_specs=(
            P("freq", None, None, "mx", "my"),
            P("freq", None, None, "mx", "my"),
            P("mx", "my"),
            P("mx", "my"),
            P("mx", "my"),
            P("freq"),
            P(("mx", "my"), None),
            P(("mx", "my"), None),
            P(("mx", "my"), None),
        ),
        out_specs=(P("freq", None, None, "mx", "my"), P("mx", "my")),
        check_vma=False,
    )
```

profile of v0, /device:TPU:98, one launch (start us, length us, event | category | flops | bytes accessed | tf_op | source)
XLA Modules:
  0.0 1374.9 jit_solution(1580240488645792618)
XLA Ops:
  13.7 11.6 scatter_custom_fusion.1
  41.8 1255.3 %while.10 = (s32[]{:T(128)}, f32[6,64,256]{2,1,0:T(8,128)S(1)}, f32[64,256]{1,0:T(8,128)S(1)}, f32[6,64,256]{2,1,0:T(8,128)}, s32[2048]{0:T(1024)}, /*index=5*/s...) while((s32[]{:T(128)}, f32[6,64,256]{2,1,0:T(8,128)S(1)}, ...), condition=%wide.region_3.0_spmd, body=%wide.region_1.0_spmd.sunk | while | flops 2109442 | bytes 9095261 | solution.py:56
  46.6 8.8 gather_fusion
  56.7 11.4 all-to-all-start
  83.9 15.2 %scatter_custom_fusion.7 = f32[6,16384]{0,1:T(8,128)} fusion(s32[2048]{0:T(1024)S(1)} %bitcast.65, f32[2048,6]{1,0:T(8,128)S(1)} %copy.34, f32[]{:T(128)} %constant.21.clone.1..sunk), kind=kCustom, calls=%fused_computation.3.clone.1 | custom fusion | flops 12288 | bytes 393220 | tf_op jit(solution)/shard_map/while/body/eval_jaxpr/scatter-add | solution.py:43
  109.8 8.8 gather_fusion
  119.9 10.9 all-to-all-start
  146.7 15.2 %scatter_custom_fusion.7 = f32[6,16384]{0,1:T(8,128)} fusion(s32[2048]{0:T(1024)S(1)} %bitcast.65, f32[2048,6]{1,0:T(8,128)S(1)} %copy.34, f32[]{:T(128)} %constant.21.clone.1..sunk), kind=kCustom, calls=%fused_computation.3.clone.1 | custom fusion | flops 12288 | bytes 393220 | tf_op jit(solution)/shard_map/while/body/eval_jaxpr/scatter-add | solution.py:43
  172.5 8.8 gather_fusion
  182.6 10.9 all-to-all-start
  209.4 15.2 %scatter_custom_fusion.7 = f32[6,16384]{0,1:T(8,128)} fusion(s32[2048]{0:T(1024)S(1)} %bitcast.65, f32[2048,6]{1,0:T(8,128)S(1)} %copy.34, f32[]{:T(128)} %constant.21.clone.1..sunk), kind=kCustom, calls=%fused_computation.3.clone.1 | custom fusion | flops 12288 | bytes 393220 | tf_op jit(solution)/shard_map/while/body/eval_jaxpr/scatter-add | solution.py:43
  235.3 8.8 gather_fusion
  245.4 10.9 all-to-all-start
  272.1 15.2 %scatter_custom_fusion.7 = f32[6,16384]{0,1:T(8,128)} fusion(s32[2048]{0:T(1024)S(1)} %bitcast.65, f32[2048,6]{1,0:T(8,128)S(1)} %copy.34, f32[]{:T(128)} %constant.21.clone.1..sunk), kind=kCustom, calls=%fused_computation.3.clone.1 | custom fusion | flops 12288 | bytes 393220 | tf_op jit(solution)/shard_map/while/body/eval_jaxpr/scatter-add | solution.py:43
  298.0 8.8 gather_fusion
  308.1 10.9 all-to-all-start
  334.9 15.2 %scatter_custom_fusion.7 = f32[6,16384]{0,1:T(8,128)} fusion(s32[2048]{0:T(1024)S(1)} %bitcast.65, f32[2048,6]{1,0:T(8,128)S(1)} %copy.34, f32[]{:T(128)} %constant.21.clone.1..sunk), kind=kCustom, calls=%fused_computation.3.clone.1 | custom fusion | flops 12288 | bytes 393220 | tf_op jit(solution)/shard_map/while/body/eval_jaxpr/scatter-add | solution.py:43
  370.8 10.9 all-to-all-start
  397.6 15.2 %scatter_custom_fusion.7 = f32[6,16384]{0,1:T(8,128)} fusion(s32[2048]{0:T(1024)S(1)} %bitcast.65, f32[2048,6]{1,0:T(8,128)S(1)} %copy.34, f32[]{:T(128)} %constant.21.clone.1..sunk), kind=kCustom, calls=%fused_computation.3.clone.1 | custom fusion | flops 12288 | bytes 393220 | tf_op jit(solution)/shard_map/while/body/eval_jaxpr/scatter-add | solution.py:43
  433.6 10.9 all-to-all-start
  460.4 15.2 %scatter_custom_fusion.7 = f32[6,16384]{0,1:T(8,128)} fusion(s32[2048]{0:T(1024)S(1)} %bitcast.65, f32[2048,6]{1,0:T(8,128)S(1)} %copy.34, f32[]{:T(128)} %constant.21.clone.1..sunk), kind=kCustom, calls=%fused_computation.3.clone.1 | custom fusion | flops 12288 | bytes 393220 | tf_op jit(solution)/shard_map/while/body/eval_jaxpr/scatter-add | solution.py:43
  496.3 10.9 all-to-all-start
  523.1 15.2 %scatter_custom_fusion.7 = f32[6,16384]{0,1:T(8,128)} fusion(s32[2048]{0:T(1024)S(1)} %bitcast.65, f32[2048,6]{1,0:T(8,128)S(1)} %copy.34, f32[]{:T(128)} %constant.21.clone.1..sunk), kind=kCustom, calls=%fused_computation.3.clone.1 | custom fusion | flops 12288 | bytes 393220 | tf_op jit(solution)/shard_map/while/body/eval_jaxpr/scatter-add | solution.py:43
  559.1 10.9 all-to-all-start
  585.8 15.2 %scatter_custom_fusion.7 = f32[6,16384]{0,1:T(8,128)} fusion(s32[2048]{0:T(1024)S(1)} %bitcast.65, f32[2048,6]{1,0:T(8,128)S(1)} %copy.34, f32[]{:T(128)} %constant.21.clone.1..sunk), kind=kCustom, calls=%fused_computation.3.clone.1 | custom fusion | flops 12288 | bytes 393220 | tf_op jit(solution)/shard_map/while/body/eval_jaxpr/scatter-add | solution.py:43
  621.8 10.9 all-to-all-start
  648.6 15.2 %scatter_custom_fusion.7 = f32[6,16384]{0,1:T(8,128)} fusion(s32[2048]{0:T(1024)S(1)} %bitcast.65, f32[2048,6]{1,0:T(8,128)S(1)} %copy.34, f32[]{:T(128)} %constant.21.clone.1..sunk), kind=kCustom, calls=%fused_computation.3.clone.1 | custom fusion | flops 12288 | bytes 393220 | tf_op jit(solution)/shard_map/while/body/eval_jaxpr/scatter-add | solution.py:43
  684.5 10.9 all-to-all-start
  711.3 15.2 %scatter_custom_fusion.7 = f32[6,16384]{0,1:T(8,128)} fusion(s32[2048]{0:T(1024)S(1)} %bitcast.65, f32[2048,6]{1,0:T(8,128)S(1)} %copy.34, f32[]{:T(128)} %constant.21.clone.1..sunk), kind=kCustom, calls=%fused_computation.3.clone.1 | custom fusion | flops 12288 | bytes 393220 | tf_op jit(solution)/shard_map/while/body/eval_jaxpr/scatter-add | solution.py:43
  747.3 10.9 all-to-all-start
  774.1 15.2 %scatter_custom_fusion.7 = f32[6,16384]{0,1:T(8,128)} fusion(s32[2048]{0:T(1024)S(1)} %bitcast.65, f32[2048,6]{1,0:T(8,128)S(1)} %copy.34, f32[]{:T(128)} %constant.21.clone.1..sunk), kind=kCustom, calls=%fused_computation.3.clone.1 | custom fusion | flops 12288 | bytes 393220 | tf_op jit(solution)/shard_map/while/body/eval_jaxpr/scatter-add | solution.py:43
  810.0 10.9 all-to-all-start
  836.8 15.2 %scatter_custom_fusion.7 = f32[6,16384]{0,1:T(8,128)} fusion(s32[2048]{0:T(1024)S(1)} %bitcast.65, f32[2048,6]{1,0:T(8,128)S(1)} %copy.34, f32[]{:T(128)} %constant.21.clone.1..sunk), kind=kCustom, calls=%fused_computation.3.clone.1 | custom fusion | flops 12288 | bytes 393220 | tf_op jit(solution)/shard_map/while/body/eval_jaxpr/scatter-add | solution.py:43
  872.8 10.9 all-to-all-start
  899.5 15.2 %scatter_custom_fusion.7 = f32[6,16384]{0,1:T(8,128)} fusion(s32[2048]{0:T(1024)S(1)} %bitcast.65, f32[2048,6]{1,0:T(8,128)S(1)} %copy.34, f32[]{:T(128)} %constant.21.clone.1..sunk), kind=kCustom, calls=%fused_computation.3.clone.1 | custom fusion | flops 12288 | bytes 393220 | tf_op jit(solution)/shard_map/while/body/eval_jaxpr/scatter-add | solution.py:43
  935.5 10.9 all-to-all-start
  962.3 15.2 %scatter_custom_fusion.7 = f32[6,16384]{0,1:T(8,128)} fusion(s32[2048]{0:T(1024)S(1)} %bitcast.65, f32[2048,6]{1,0:T(8,128)S(1)} %copy.34, f32[]{:T(128)} %constant.21.clone.1..sunk), kind=kCustom, calls=%fused_computation.3.clone.1 | custom fusion | flops 12288 | bytes 393220 | tf_op jit(solution)/shard_map/while/body/eval_jaxpr/scatter-add | solution.py:43
  998.2 10.9 all-to-all-start
  1025.0 15.2 %scatter_custom_fusion.7 = f32[6,16384]{0,1:T(8,128)} fusion(s32[2048]{0:T(1024)S(1)} %bitcast.65, f32[2048,6]{1,0:T(8,128)S(1)} %copy.34, f32[]{:T(128)} %constant.21.clone.1..sunk), kind=kCustom, calls=%fused_computation.3.clone.1 | custom fusion | flops 12288 | bytes 393220 | tf_op jit(solution)/shard_map/while/body/eval_jaxpr/scatter-add | solution.py:43
  1061.0 10.9 all-to-all-start
  1087.8 15.2 %scatter_custom_fusion.7 = f32[6,16384]{0,1:T(8,128)} fusion(s32[2048]{0:T(1024)S(1)} %bitcast.65, f32[2048,6]{1,0:T(8,128)S(1)} %copy.34, f32[]{:T(128)} %constant.21.clone.1..sunk), kind=kCustom, calls=%fused_computation.3.clone.1 | custom fusion | flops 12288 | bytes 393220 | tf_op jit(solution)/shard_map/while/body/eval_jaxpr/scatter-add | solution.py:43
  1123.7 10.9 all-to-all-start
  1150.5 15.2 %scatter_custom_fusion.7 = f32[6,16384]{0,1:T(8,128)} fusion(s32[2048]{0:T(1024)S(1)} %bitcast.65, f32[2048,6]{1,0:T(8,128)S(1)} %copy.34, f32[]{:T(128)} %constant.21.clone.1..sunk), kind=kCustom, calls=%fused_computation.3.clone.1 | custom fusion | flops 12288 | bytes 393220 | tf_op jit(solution)/shard_map/while/body/eval_jaxpr/scatter-add | solution.py:43
  1186.5 10.9 all-to-all-start
  1213.2 15.2 %scatter_custom_fusion.7 = f32[6,16384]{0,1:T(8,128)} fusion(s32[2048]{0:T(1024)S(1)} %bitcast.65, f32[2048,6]{1,0:T(8,128)S(1)} %copy.34, f32[]{:T(128)} %constant.21.clone.1..sunk), kind=kCustom, calls=%fused_computation.3.clone.1 | custom fusion | flops 12288 | bytes 393220 | tf_op jit(solution)/shard_map/while/body/eval_jaxpr/scatter-add | solution.py:43
  1249.2 10.9 all-to-all-start
  1276.0 15.2 %scatter_custom_fusion.7 = f32[6,16384]{0,1:T(8,128)} fusion(s32[2048]{0:T(1024)S(1)} %bitcast.65, f32[2048,6]{1,0:T(8,128)S(1)} %copy.34, f32[]{:T(128)} %constant.21.clone.1..sunk), kind=kCustom, calls=%fused_computation.3.clone.1 | custom fusion | flops 12288 | bytes 393220 | tf_op jit(solution)/shard_map/while/body/eval_jaxpr/scatter-add | solution.py:43
  1299.1 48.6 %all-reduce.2.cloned.1.call-done = f32[64,256]{1,0:T(8,128)} async-done(((f32[64,256]{1,0:T(8,128)}), f32[64,256]{1,0:T(8,128)}) %all-reduce.2.cloned.1.call-update) | async-done | bytes 65552 | tf_op jit(solution)/shard_map/psum | solution.py:71
  (798 shorter events, 727.4 us)
Async XLA Ops:
  7.2 1340.5 %all-reduce.2.cloned.1.call-start = ((), (), s32[]{:S(2)}) async-start(), calls=%async_computation.1 | async-start | bytes 131072 | tf_op jit(solution)/shard_map/psum | solution.py:71
  56.7 25.2 %all-to-all-start = ((f32[64,1,192]{2,1,0:T(1,128)}), f32[64,1,192]{2,1,0:T(1,128)S(1)}, u32[]{:S(2)}, u32[]{:S(2)}) async-start(f32[64,1,192]{2,1,0:T(1,128)} %reshape.136), calls=%async_computation | async-start | bytes 131072 | tf_op jit(solution)/shard_map/while/body/eval_jaxpr/all_to_all | solution.py:42
  75.4 29.1 %collective-permute-start.2 = (f32[6,66,1]{2,1,0:T(8,128)S(1)}, f32[6,66,1]{2,1,0:T(8,128)S(1)}, u32[]{:S(2)}, u32[]{:S(2)}) collective-permute-start(f32[6,66,1]{2,1,0:T(8,128)S(1)} %get-tuple-element.180), channel_id=1, source_target_pairs={{0,1},{1,2},{2,3},{3,4},{4,5},{5,6},{6,7},{8,9},{9,10},{10,11},{11... | collective-permute-start | bytes 4760 | tf_op jit(solution)/shard_map/while/body/eval_jaxpr/ppermute | solution.py:16
  80.0 24.5 %collective-permute-start.3 = (f32[6,66,1]{2,1,0:T(8,128)S(1)}, f32[6,66,1]{2,1,0:T(8,128)S(1)}, u32[]{:S(2)}, u32[]{:S(2)}) collective-permute-start(f32[6,66,1]{2,1,0:T(8,128)S(1)} %get-tuple-element.181), channel_id=1, source_target_pairs={{1,0},{2,1},{3,2},{4,3},{5,4},{6,5},{7,6},{9,8},{10,9},{11,10},{12... | collective-permute-start | bytes 4760 | tf_op jit(solution)/shard_map/while/body/eval_jaxpr/ppermute | solution.py:17
  119.9 24.8 %all-to-all-start = ((f32[64,1,192]{2,1,0:T(1,128)}), f32[64,1,192]{2,1,0:T(1,128)S(1)}, u32[]{:S(2)}, u32[]{:S(2)}) async-start(f32[64,1,192]{2,1,0:T(1,128)} %reshape.136), calls=%async_computation | async-start | bytes 131072 | tf_op jit(solution)/shard_map/while/body/eval_jaxpr/all_to_all | solution.py:42
  138.1 29.1 %collective-permute-start.2 = (f32[6,66,1]{2,1,0:T(8,128)S(1)}, f32[6,66,1]{2,1,0:T(8,128)S(1)}, u32[]{:S(2)}, u32[]{:S(2)}) collective-permute-start(f32[6,66,1]{2,1,0:T(8,128)S(1)} %get-tuple-element.180), channel_id=1, source_target_pairs={{0,1},{1,2},{2,3},{3,4},{4,5},{5,6},{6,7},{8,9},{9,10},{10,11},{11... | collective-permute-start | bytes 4760 | tf_op jit(solution)/shard_map/while/body/eval_jaxpr/ppermute | solution.py:16
  142.7 24.5 %collective-permute-start.3 = (f32[6,66,1]{2,1,0:T(8,128)S(1)}, f32[6,66,1]{2,1,0:T(8,128)S(1)}, u32[]{:S(2)}, u32[]{:S(2)}) collective-permute-start(f32[6,66,1]{2,1,0:T(8,128)S(1)} %get-tuple-element.181), channel_id=1, source_target_pairs={{1,0},{2,1},{3,2},{4,3},{5,4},{6,5},{7,6},{9,8},{10,9},{11,10},{12... | collective-permute-start | bytes 4760 | tf_op jit(solution)/shard_map/while/body/eval_jaxpr/ppermute | solution.py:17
  182.6 24.8 %all-to-all-start = ((f32[64,1,192]{2,1,0:T(1,128)}), f32[64,1,192]{2,1,0:T(1,128)S(1)}, u32[]{:S(2)}, u32[]{:S(2)}) async-start(f32[64,1,192]{2,1,0:T(1,128)} %reshape.136), calls=%async_computation | async-start | bytes 131072 | tf_op jit(solution)/shard_map/while/body/eval_jaxpr/all_to_all | solution.py:42
  200.9 29.1 %collective-permute-start.2 = (f32[6,66,1]{2,1,0:T(8,128)S(1)}, f32[6,66,1]{2,1,0:T(8,128)S(1)}, u32[]{:S(2)}, u32[]{:S(2)}) collective-permute-start(f32[6,66,1]{2,1,0:T(8,128)S(1)} %get-tuple-element.180), channel_id=1, source_target_pairs={{0,1},{1,2},{2,3},{3,4},{4,5},{5,6},{6,7},{8,9},{9,10},{10,11},{11... | collective-permute-start | bytes 4760 | tf_op jit(solution)/shard_map/while/body/eval_jaxpr/ppermute | solution.py:16
  205.5 24.5 %collective-permute-start.3 = (f32[6,66,1]{2,1,0:T(8,128)S(1)}, f32[6,66,1]{2,1,0:T(8,128)S(1)}, u32[]{:S(2)}, u32[]{:S(2)}) collective-permute-start(f32[6,66,1]{2,1,0:T(8,128)S(1)} %get-tuple-element.181), channel_id=1, source_target_pairs={{1,0},{2,1},{3,2},{4,3},{5,4},{6,5},{7,6},{9,8},{10,9},{11,10},{12... | collective-permute-start | bytes 4760 | tf_op jit(solution)/shard_map/while/body/eval_jaxpr/ppermute | solution.py:17
  245.4 24.8 %all-to-all-start = ((f32[64,1,192]{2,1,0:T(1,128)}), f32[64,1,192]{2,1,0:T(1,128)S(1)}, u32[]{:S(2)}, u32[]{:S(2)}) async-start(f32[64,1,192]{2,1,0:T(1,128)} %reshape.136), calls=%async_computation | async-start | bytes 131072 | tf_op jit(solution)/shard_map/while/body/eval_jaxpr/all_to_all | solution.py:42
  263.6 29.1 %collective-permute-start.2 = (f32[6,66,1]{2,1,0:T(8,128)S(1)}, f32[6,66,1]{2,1,0:T(8,128)S(1)}, u32[]{:S(2)}, u32[]{:S(2)}) collective-permute-start(f32[6,66,1]{2,1,0:T(8,128)S(1)} %get-tuple-element.180), channel_id=1, source_target_pairs={{0,1},{1,2},{2,3},{3,4},{4,5},{5,6},{6,7},{8,9},{9,10},{10,11},{11... | collective-permute-start | bytes 4760 | tf_op jit(solution)/shard_map/while/body/eval_jaxpr/ppermute | solution.py:16
  268.2 24.5 %collective-permute-start.3 = (f32[6,66,1]{2,1,0:T(8,128)S(1)}, f32[6,66,1]{2,1,0:T(8,128)S(1)}, u32[]{:S(2)}, u32[]{:S(2)}) collective-permute-start(f32[6,66,1]{2,1,0:T(8,128)S(1)} %get-tuple-element.181), channel_id=1, source_target_pairs={{1,0},{2,1},{3,2},{4,3},{5,4},{6,5},{7,6},{9,8},{10,9},{11,10},{12... | collective-permute-start | bytes 4760 | tf_op jit(solution)/shard_map/while/body/eval_jaxpr/ppermute | solution.py:17
  308.1 24.8 %all-to-all-start = ((f32[64,1,192]{2,1,0:T(1,128)}), f32[64,1,192]{2,1,0:T(1,128)S(1)}, u32[]{:S(2)}, u32[]{:S(2)}) async-start(f32[64,1,192]{2,1,0:T(1,128)} %reshape.136), calls=%async_computation | async-start | bytes 131072 | tf_op jit(solution)/shard_map/while/body/eval_jaxpr/all_to_all | solution.py:42
  326.4 29.1 %collective-permute-start.2 = (f32[6,66,1]{2,1,0:T(8,128)S(1)}, f32[6,66,1]{2,1,0:T(8,128)S(1)}, u32[]{:S(2)}, u32[]{:S(2)}) collective-permute-start(f32[6,66,1]{2,1,0:T(8,128)S(1)} %get-tuple-element.180), channel_id=1, source_target_pairs={{0,1},{1,2},{2,3},{3,4},{4,5},{5,6},{6,7},{8,9},{9,10},{10,11},{11... | collective-permute-start | bytes 4760 | tf_op jit(solution)/shard_map/while/body/eval_jaxpr/ppermute | solution.py:16
  330.9 24.5 %collective-permute-start.3 = (f32[6,66,1]{2,1,0:T(8,128)S(1)}, f32[6,66,1]{2,1,0:T(8,128)S(1)}, u32[]{:S(2)}, u32[]{:S(2)}) collective-permute-start(f32[6,66,1]{2,1,0:T(8,128)S(1)} %get-tuple-element.181), channel_id=1, source_target_pairs={{1,0},{2,1},{3,2},{4,3},{5,4},{6,5},{7,6},{9,8},{10,9},{11,10},{12... | collective-permute-start | bytes 4760 | tf_op jit(solution)/shard_map/while/body/eval_jaxpr/ppermute | solution.py:17
  370.8 24.8 %all-to-all-start = ((f32[64,1,192]{2,1,0:T(1,128)}), f32[64,1,192]{2,1,0:T(1,128)S(1)}, u32[]{:S(2)}, u32[]{:S(2)}) async-start(f32[64,1,192]{2,1,0:T(1,128)} %reshape.136), calls=%async_computation | async-start | bytes 131072 | tf_op jit(solution)/shard_map/while/body/eval_jaxpr/all_to_all | solution.py:42
  389.1 29.1 %collective-permute-start.2 = (f32[6,66,1]{2,1,0:T(8,128)S(1)}, f32[6,66,1]{2,1,0:T(8,128)S(1)}, u32[]{:S(2)}, u32[]{:S(2)}) collective-permute-start(f32[6,66,1]{2,1,0:T(8,128)S(1)} %get-tuple-element.180), channel_id=1, source_target_pairs={{0,1},{1,2},{2,3},{3,4},{4,5},{5,6},{6,7},{8,9},{9,10},{10,11},{11... | collective-permute-start | bytes 4760 | tf_op jit(solution)/shard_map/while/body/eval_jaxpr/ppermute | solution.py:16
  393.7 24.5 %collective-permute-start.3 = (f32[6,66,1]{2,1,0:T(8,128)S(1)}, f32[6,66,1]{2,1,0:T(8,128)S(1)}, u32[]{:S(2)}, u32[]{:S(2)}) collective-permute-start(f32[6,66,1]{2,1,0:T(8,128)S(1)} %get-tuple-element.181), channel_id=1, source_target_pairs={{1,0},{2,1},{3,2},{4,3},{5,4},{6,5},{7,6},{9,8},{10,9},{11,10},{12... | collective-permute-start | bytes 4760 | tf_op jit(solution)/shard_map/while/body/eval_jaxpr/ppermute | solution.py:17
  433.6 24.8 %all-to-all-start = ((f32[64,1,192]{2,1,0:T(1,128)}), f32[64,1,192]{2,1,0:T(1,128)S(1)}, u32[]{:S(2)}, u32[]{:S(2)}) async-start(f32[64,1,192]{2,1,0:T(1,128)} %reshape.136), calls=%async_computation | async-start | bytes 131072 | tf_op jit(solution)/shard_map/while/body/eval_jaxpr/all_to_all | solution.py:42
  451.8 29.1 %collective-permute-start.2 = (f32[6,66,1]{2,1,0:T(8,128)S(1)}, f32[6,66,1]{2,1,0:T(8,128)S(1)}, u32[]{:S(2)}, u32[]{:S(2)}) collective-permute-start(f32[6,66,1]{2,1,0:T(8,128)S(1)} %get-tuple-element.180), channel_id=1, source_target_pairs={{0,1},{1,2},{2,3},{3,4},{4,5},{5,6},{6,7},{8,9},{9,10},{10,11},{11... | collective-permute-start | bytes 4760 | tf_op jit(solution)/shard_map/while/body/eval_jaxpr/ppermute | solution.py:16
  456.4 24.5 %collective-permute-start.3 = (f32[6,66,1]{2,1,0:T(8,128)S(1)}, f32[6,66,1]{2,1,0:T(8,128)S(1)}, u32[]{:S(2)}, u32[]{:S(2)}) collective-permute-start(f32[6,66,1]{2,1,0:T(8,128)S(1)} %get-tuple-element.181), channel_id=1, source_target_pairs={{1,0},{2,1},{3,2},{4,3},{5,4},{6,5},{7,6},{9,8},{10,9},{11,10},{12... | collective-permute-start | bytes 4760 | tf_op jit(solution)/shard_map/while/body/eval_jaxpr/ppermute | solution.py:17
  496.3 24.8 %all-to-all-start = ((f32[64,1,192]{2,1,0:T(1,128)}), f32[64,1,192]{2,1,0:T(1,128)S(1)}, u32[]{:S(2)}, u32[]{:S(2)}) async-start(f32[64,1,192]{2,1,0:T(1,128)} %reshape.136), calls=%async_computation | async-start | bytes 131072 | tf_op jit(solution)/shard_map/while/body/eval_jaxpr/all_to_all | solution.py:42
  514.6 29.1 %collective-permute-start.2 = (f32[6,66,1]{2,1,0:T(8,128)S(1)}, f32[6,66,1]{2,1,0:T(8,128)S(1)}, u32[]{:S(2)}, u32[]{:S(2)}) collective-permute-start(f32[6,66,1]{2,1,0:T(8,128)S(1)} %get-tuple-element.180), channel_id=1, source_target_pairs={{0,1},{1,2},{2,3},{3,4},{4,5},{5,6},{6,7},{8,9},{9,10},{10,11},{11... | collective-permute-start | bytes 4760 | tf_op jit(solution)/shard_map/while/body/eval_jaxpr/ppermute | solution.py:16
  559.1 24.8 %all-to-all-start = ((f32[64,1,192]{2,1,0:T(1,128)}), f32[64,1,192]{2,1,0:T(1,128)S(1)}, u32[]{:S(2)}, u32[]{:S(2)}) async-start(f32[64,1,192]{2,1,0:T(1,128)} %reshape.136), calls=%async_computation | async-start | bytes 131072 | tf_op jit(solution)/shard_map/while/body/eval_jaxpr/all_to_all | solution.py:42
  577.3 29.1 %collective-permute-start.2 = (f32[6,66,1]{2,1,0:T(8,128)S(1)}, f32[6,66,1]{2,1,0:T(8,128)S(1)}, u32[]{:S(2)}, u32[]{:S(2)}) collective-permute-start(f32[6,66,1]{2,1,0:T(8,128)S(1)} %get-tuple-element.180), channel_id=1, source_target_pairs={{0,1},{1,2},{2,3},{3,4},{4,5},{5,6},{6,7},{8,9},{9,10},{10,11},{11... | collective-permute-start | bytes 4760 | tf_op jit(solution)/shard_map/while/body/eval_jaxpr/ppermute | solution.py:16
  621.8 24.8 %all-to-all-start = ((f32[64,1,192]{2,1,0:T(1,128)}), f32[64,1,192]{2,1,0:T(1,128)S(1)}, u32[]{:S(2)}, u32[]{:S(2)}) async-start(f32[64,1,192]{2,1,0:T(1,128)} %reshape.136), calls=%async_computation | async-start | bytes 131072 | tf_op jit(solution)/shard_map/while/body/eval_jaxpr/all_to_all | solution.py:42
  640.1 29.1 %collective-permute-start.2 = (f32[6,66,1]{2,1,0:T(8,128)S(1)}, f32[6,66,1]{2,1,0:T(8,128)S(1)}, u32[]{:S(2)}, u32[]{:S(2)}) collective-permute-start(f32[6,66,1]{2,1,0:T(8,128)S(1)} %get-tuple-element.180), channel_id=1, source_target_pairs={{0,1},{1,2},{2,3},{3,4},{4,5},{5,6},{6,7},{8,9},{9,10},{10,11},{11... | collective-permute-start | bytes 4760 | tf_op jit(solution)/shard_map/while/body/eval_jaxpr/ppermute | solution.py:16
  684.5 24.8 %all-to-all-start = ((f32[64,1,192]{2,1,0:T(1,128)}), f32[64,1,192]{2,1,0:T(1,128)S(1)}, u32[]{:S(2)}, u32[]{:S(2)}) async-start(f32[64,1,192]{2,1,0:T(1,128)} %reshape.136), calls=%async_computation | async-start | bytes 131072 | tf_op jit(solution)/shard_map/while/body/eval_jaxpr/all_to_all | solution.py:42
  702.8 29.1 %collective-permute-start.2 = (f32[6,66,1]{2,1,0:T(8,128)S(1)}, f32[6,66,1]{2,1,0:T(8,128)S(1)}, u32[]{:S(2)}, u32[]{:S(2)}) collective-permute-start(f32[6,66,1]{2,1,0:T(8,128)S(1)} %get-tuple-element.180), channel_id=1, source_target_pairs={{0,1},{1,2},{2,3},{3,4},{4,5},{5,6},{6,7},{8,9},{9,10},{10,11},{11... | collective-permute-start | bytes 4760 | tf_op jit(solution)/shard_map/while/body/eval_jaxpr/ppermute | solution.py:16
  747.3 24.8 %all-to-all-start = ((f32[64,1,192]{2,1,0:T(1,128)}), f32[64,1,192]{2,1,0:T(1,128)S(1)}, u32[]{:S(2)}, u32[]{:S(2)}) async-start(f32[64,1,192]{2,1,0:T(1,128)} %reshape.136), calls=%async_computation | async-start | bytes 131072 | tf_op jit(solution)/shard_map/while/body/eval_jaxpr/all_to_all | solution.py:42
  765.5 29.1 %collective-permute-start.2 = (f32[6,66,1]{2,1,0:T(8,128)S(1)}, f32[6,66,1]{2,1,0:T(8,128)S(1)}, u32[]{:S(2)}, u32[]{:S(2)}) collective-permute-start(f32[6,66,1]{2,1,0:T(8,128)S(1)} %get-tuple-element.180), channel_id=1, source_target_pairs={{0,1},{1,2},{2,3},{3,4},{4,5},{5,6},{6,7},{8,9},{9,10},{10,11},{11... | collective-permute-start | bytes 4760 | tf_op jit(solution)/shard_map/while/body/eval_jaxpr/ppermute | solution.py:16
  810.0 24.8 %all-to-all-start = ((f32[64,1,192]{2,1,0:T(1,128)}), f32[64,1,192]{2,1,0:T(1,128)S(1)}, u32[]{:S(2)}, u32[]{:S(2)}) async-start(f32[64,1,192]{2,1,0:T(1,128)} %reshape.136), calls=%async_computation | async-start | bytes 131072 | tf_op jit(solution)/shard_map/while/body/eval_jaxpr/all_to_all | solution.py:42
  828.3 29.1 %collective-permute-start.2 = (f32[6,66,1]{2,1,0:T(8,128)S(1)}, f32[6,66,1]{2,1,0:T(8,128)S(1)}, u32[]{:S(2)}, u32[]{:S(2)}) collective-permute-start(f32[6,66,1]{2,1,0:T(8,128)S(1)} %get-tuple-element.180), channel_id=1, source_target_pairs={{0,1},{1,2},{2,3},{3,4},{4,5},{5,6},{6,7},{8,9},{9,10},{10,11},{11... | collective-permute-start | bytes 4760 | tf_op jit(solution)/shard_map/while/body/eval_jaxpr/ppermute | solution.py:16
  872.8 24.8 %all-to-all-start = ((f32[64,1,192]{2,1,0:T(1,128)}), f32[64,1,192]{2,1,0:T(1,128)S(1)}, u32[]{:S(2)}, u32[]{:S(2)}) async-start(f32[64,1,192]{2,1,0:T(1,128)} %reshape.136), calls=%async_computation | async-start | bytes 131072 | tf_op jit(solution)/shard_map/while/body/eval_jaxpr/all_to_all | solution.py:42
  891.0 29.1 %collective-permute-start.2 = (f32[6,66,1]{2,1,0:T(8,128)S(1)}, f32[6,66,1]{2,1,0:T(8,128)S(1)}, u32[]{:S(2)}, u32[]{:S(2)}) collective-permute-start(f32[6,66,1]{2,1,0:T(8,128)S(1)} %get-tuple-element.180), channel_id=1, source_target_pairs={{0,1},{1,2},{2,3},{3,4},{4,5},{5,6},{6,7},{8,9},{9,10},{10,11},{11... | collective-permute-start | bytes 4760 | tf_op jit(solution)/shard_map/while/body/eval_jaxpr/ppermute | solution.py:16
  935.5 24.8 %all-to-all-start = ((f32[64,1,192]{2,1,0:T(1,128)}), f32[64,1,192]{2,1,0:T(1,128)S(1)}, u32[]{:S(2)}, u32[]{:S(2)}) async-start(f32[64,1,192]{2,1,0:T(1,128)} %reshape.136), calls=%async_computation | async-start | bytes 131072 | tf_op jit(solution)/shard_map/while/body/eval_jaxpr/all_to_all | solution.py:42
  953.8 29.1 %collective-permute-start.2 = (f32[6,66,1]{2,1,0:T(8,128)S(1)}, f32[6,66,1]{2,1,0:T(8,128)S(1)}, u32[]{:S(2)}, u32[]{:S(2)}) collective-permute-start(f32[6,66,1]{2,1,0:T(8,128)S(1)} %get-tuple-element.180), channel_id=1, source_target_pairs={{0,1},{1,2},{2,3},{3,4},{4,5},{5,6},{6,7},{8,9},{9,10},{10,11},{11... | collective-permute-start | bytes 4760 | tf_op jit(solution)/shard_map/while/body/eval_jaxpr/ppermute | solution.py:16
  998.2 24.8 %all-to-all-start = ((f32[64,1,192]{2,1,0:T(1,128)}), f32[64,1,192]{2,1,0:T(1,128)S(1)}, u32[]{:S(2)}, u32[]{:S(2)}) async-start(f32[64,1,192]{2,1,0:T(1,128)} %reshape.136), calls=%async_computation | async-start | bytes 131072 | tf_op jit(solution)/shard_map/while/body/eval_jaxpr/all_to_all | solution.py:42
  1016.5 29.1 %collective-permute-start.2 = (f32[6,66,1]{2,1,0:T(8,128)S(1)}, f32[6,66,1]{2,1,0:T(8,128)S(1)}, u32[]{:S(2)}, u32[]{:S(2)}) collective-permute-start(f32[6,66,1]{2,1,0:T(8,128)S(1)} %get-tuple-element.180), channel_id=1, source_target_pairs={{0,1},{1,2},{2,3},{3,4},{4,5},{5,6},{6,7},{8,9},{9,10},{10,11},{11... | collective-permute-start | bytes 4760 | tf_op jit(solution)/shard_map/while/body/eval_jaxpr/ppermute | solution.py:16
  1061.0 24.8 %all-to-all-start = ((f32[64,1,192]{2,1,0:T(1,128)}), f32[64,1,192]{2,1,0:T(1,128)S(1)}, u32[]{:S(2)}, u32[]{:S(2)}) async-start(f32[64,1,192]{2,1,0:T(1,128)} %reshape.136), calls=%async_computation | async-start | bytes 131072 | tf_op jit(solution)/shard_map/while/body/eval_jaxpr/all_to_all | solution.py:42
  1079.2 29.1 %collective-permute-start.2 = (f32[6,66,1]{2,1,0:T(8,128)S(1)}, f32[6,66,1]{2,1,0:T(8,128)S(1)}, u32[]{:S(2)}, u32[]{:S(2)}) collective-permute-start(f32[6,66,1]{2,1,0:T(8,128)S(1)} %get-tuple-element.180), channel_id=1, source_target_pairs={{0,1},{1,2},{2,3},{3,4},{4,5},{5,6},{6,7},{8,9},{9,10},{10,11},{11... | collective-permute-start | bytes 4760 | tf_op jit(solution)/shard_map/while/body/eval_jaxpr/ppermute | solution.py:16
  1123.7 24.8 %all-to-all-start = ((f32[64,1,192]{2,1,0:T(1,128)}), f32[64,1,192]{2,1,0:T(1,128)S(1)}, u32[]{:S(2)}, u32[]{:S(2)}) async-start(f32[64,1,192]{2,1,0:T(1,128)} %reshape.136), calls=%async_computation | async-start | bytes 131072 | tf_op jit(solution)/shard_map/while/body/eval_jaxpr/all_to_all | solution.py:42
  1142.0 29.1 %collective-permute-start.2 = (f32[6,66,1]{2,1,0:T(8,128)S(1)}, f32[6,66,1]{2,1,0:T(8,128)S(1)}, u32[]{:S(2)}, u32[]{:S(2)}) collective-permute-start(f32[6,66,1]{2,1,0:T(8,128)S(1)} %get-tuple-element.180), channel_id=1, source_target_pairs={{0,1},{1,2},{2,3},{3,4},{4,5},{5,6},{6,7},{8,9},{9,10},{10,11},{11... | collective-permute-start | bytes 4760 | tf_op jit(solution)/shard_map/while/body/eval_jaxpr/ppermute | solution.py:16
  1186.5 24.8 %all-to-all-start = ((f32[64,1,192]{2,1,0:T(1,128)}), f32[64,1,192]{2,1,0:T(1,128)S(1)}, u32[]{:S(2)}, u32[]{:S(2)}) async-start(f32[64,1,192]{2,1,0:T(1,128)} %reshape.136), calls=%async_computation | async-start | bytes 131072 | tf_op jit(solution)/shard_map/while/body/eval_jaxpr/all_to_all | solution.py:42
  1204.7 29.1 %collective-permute-start.2 = (f32[6,66,1]{2,1,0:T(8,128)S(1)}, f32[6,66,1]{2,1,0:T(8,128)S(1)}, u32[]{:S(2)}, u32[]{:S(2)}) collective-permute-start(f32[6,66,1]{2,1,0:T(8,128)S(1)} %get-tuple-element.180), channel_id=1, source_target_pairs={{0,1},{1,2},{2,3},{3,4},{4,5},{5,6},{6,7},{8,9},{9,10},{10,11},{11... | collective-permute-start | bytes 4760 | tf_op jit(solution)/shard_map/while/body/eval_jaxpr/ppermute | solution.py:16
  1249.2 24.8 %all-to-all-start = ((f32[64,1,192]{2,1,0:T(1,128)}), f32[64,1,192]{2,1,0:T(1,128)S(1)}, u32[]{:S(2)}, u32[]{:S(2)}) async-start(f32[64,1,192]{2,1,0:T(1,128)} %reshape.136), calls=%async_computation | async-start | bytes 131072 | tf_op jit(solution)/shard_map/while/body/eval_jaxpr/all_to_all | solution.py:42
  1267.5 29.1 %collective-permute-start.2 = (f32[6,66,1]{2,1,0:T(8,128)S(1)}, f32[6,66,1]{2,1,0:T(8,128)S(1)}, u32[]{:S(2)}, u32[]{:S(2)}) collective-permute-start(f32[6,66,1]{2,1,0:T(8,128)S(1)} %get-tuple-element.180), channel_id=1, source_target_pairs={{0,1},{1,2},{2,3},{3,4},{4,5},{5,6},{6,7},{8,9},{9,10},{10,11},{11... | collective-permute-start | bytes 4760 | tf_op jit(solution)/shard_map/while/body/eval_jaxpr/ppermute | solution.py:16
  (144 other events, 3909.9 us)
Sparse Core Ops, SparseCore 0:
  1299.2 48.4 all-reduce.1
where the time goes:
time: 1380 us; the launch traced here: 1370 us
  starting transfers between devices  458 us (33%)
  local copies, waits for them, and re-layouts  429 us (31%)
  other arithmetic  355 us (26%)
  waiting for transfers between devices  113 us (8%)
  between operations  14.9 us (1%)
    scatter-add x20, other arithmetic, mortar(): added = jnp.zeros((6, cells), jnp.float32).at[:, targets].add(got * weights)  304 us
    all_to_all x20, starting transfers between devices, mortar(): lax.all_to_all(sent, ('mx', 'my'), split_axis=1, concat_axis=1, tiled=True)  219 us
    gather x20, local copies, waits for them, and re-layouts, mortar(): sent = field.reshape(6, cells)[:, sources]  177 us
    ppermute x44, starting transfers between devices, extended(): before = lax.ppermute(last, axis, up)  149 us
    reshape x20, local copies, waits for them, and re-layouts, mortar(): return added.reshape(6, rows_x, rows_y)  106 us
    another operation x20, local copies, waits for them, and re-layouts  94.6 us
    ppermute x44, starting transfers between devices, extended(): after = lax.ppermute(first, axis, down)  89.9 us
    ppermute x44, waiting for transfers between devices, extended(): before = lax.ppermute(last, axis, up)  59.5 us
  transfers between devices with their start and end apart: 109, of which 25 were waited for; matrix products, arithmetic and copies ran while one was open for 34% of the time, Pallas kernels for 0%

commit v1 on v0

--- a/solution.py
+++ b/solution.py
@@ -1,9 +1,21 @@
+import functools
 import jax
 import jax.numpy as jnp
 from jax import lax
 from jax.sharding import PartitionSpec as P
 
 ITERS = 20
+
+
+def perform_column(x_part, across):
+    fan = lax.axis_size(across)
+    heard = x_part
+    for kk in [[(b, b ^ tick) for b in range(fan)] for tick in (1, 2, 4, 8, 16) if tick < fan]:
+        heard = heard + lax.ppermute(heard, axis_name=across, perm=kk)
+    return heard
+
+
+end_the_yards = functools.partial(perform_column, across="freq")
 
 
 def extended(x, sides, width):
@@ -68,7 +80,7 @@
     t_re = da * u[:3] - db * u[3:] - dstiff * nb[:3]
     t_im = da * u[3:] + db * u[:3] - dstiff * nb[3:]
     sens = -jnp.sum(field[:3] * t_re - field[3:] * t_im, axis=0)
-    total = lax.psum(sens, "freq")
+    total = end_the_yards(sens)
     weighted = extended(density * total, (("mx", 0), ("my", 1)), 1)
     filt = weighted[1:-1, 1:-1]
     filt = filt + 0.5 * (

time: 1380 us -> 1330 us (0.964)
  waiting for transfers between devices: 113 us -> 70.1 us
    psum x1 -> x0, waiting for transfers between devices: 48.6 us -> none  [on_device(): total = lax.psum(sens, 'freq')]
  transfers between devices with their start and end apart: 109 -> 110, of which waited for: 25 -> 26; matrix products, arithmetic and copies ran while one was open for 34% -> 35% of each run, Pallas kernels for 0% -> 0%
where the time goes in v1:
time: 1330 us; the launch traced here: 1320 us
  starting transfers between devices  463 us (35%)
  local copies, waits for them, and re-layouts  429 us (32%)
  other arithmetic  355 us (27%)
  waiting for transfers between devices  70.1 us (5%)
    scatter-add x20, other arithmetic, mortar(): added = jnp.zeros((6, cells), jnp.float32).at[:, targets].add(got * weights)  304 us
    all_to_all x20, starting transfers between devices, mortar(): lax.all_to_all(sent, ('mx', 'my'), split_axis=1, concat_axis=1, tiled=True)  219 us
    gather x20, local copies, waits for them, and re-layouts, mortar(): sent = field.reshape(6, cells)[:, sources]  177 us
    ppermute x44, starting transfers between devices, extended(): before = lax.ppermute(last, axis, up)  149 us
    reshape x20, local copies, waits for them, and re-layouts, mortar(): return added.reshape(6, rows_x, rows_y)  106 us
    another operation x20, local copies, waits for them, and re-layouts  94.6 us
    ppermute x44, starting transfers between devices, extended(): after = lax.ppermute(first, axis, down)  89.9 us
    ppermute x44, waiting for transfers between devices, extended(): before = lax.ppermute(last, axis, up)  59.5 us
  transfers between devices with their start and end apart: 110, of which 26 were waited for; matrix products, arithmetic and copies ran while one was open for 35% of the time, Pallas kernels for 0%

profile of v1, /device:TPU:98, one launch (start us, length us, event | category | flops | bytes accessed | tf_op | source)
XLA Modules:
  0.0 1323.7 jit_solution(1392814870038724644)
XLA Ops:
  7.1 11.6 scatter_custom_fusion.1
  35.1 1255.2 %while.10 = (s32[]{:T(128)}, f32[6,64,256]{2,1,0:T(8,128)S(1)}, f32[64,256]{1,0:T(8,128)S(1)}, f32[6,64,256]{2,1,0:T(8,128)}, s32[2048]{0:T(1024)}, /*index=5*/s...) while((s32[]{:T(128)}, f32[6,64,256]{2,1,0:T(8,128)S(1)}, ...), condition=%wide.region_3.0_spmd, body=%wide.region_1.0_spmd.sunk | while | flops 2109442 | bytes 9095261 | solution.py:68
  50.1 11.4 all-to-all-start
  77.3 15.2 %scatter_custom_fusion.7 = f32[6,16384]{0,1:T(8,128)} fusion(s32[2048]{0:T(1024)S(1)} %bitcast.65, f32[2048,6]{1,0:T(8,128)S(1)} %copy.34, f32[]{:T(128)} %constant.21.clone.1..sunk), kind=kCustom, calls=%fused_computation.3.clone.1 | custom fusion | flops 12288 | bytes 393220 | tf_op jit(solution)/shard_map/while/body/eval_jaxpr/scatter-add | solution.py:55
  103.2 8.8 gather_fusion
  113.3 10.9 all-to-all-start
  140.0 15.2 %scatter_custom_fusion.7 = f32[6,16384]{0,1:T(8,128)} fusion(s32[2048]{0:T(1024)S(1)} %bitcast.65, f32[2048,6]{1,0:T(8,128)S(1)} %copy.34, f32[]{:T(128)} %constant.21.clone.1..sunk), kind=kCustom, calls=%fused_computation.3.clone.1 | custom fusion | flops 12288 | bytes 393220 | tf_op jit(solution)/shard_map/while/body/eval_jaxpr/scatter-add | solution.py:55
  176.0 10.9 all-to-all-start
  202.8 15.2 %scatter_custom_fusion.7 = f32[6,16384]{0,1:T(8,128)} fusion(s32[2048]{0:T(1024)S(1)} %bitcast.65, f32[2048,6]{1,0:T(8,128)S(1)} %copy.34, f32[]{:T(128)} %constant.21.clone.1..sunk), kind=kCustom, calls=%fused_computation.3.clone.1 | custom fusion | flops 12288 | bytes 393220 | tf_op jit(solution)/shard_map/while/body/eval_jaxpr/scatter-add | solution.py:55
  238.7 10.9 all-to-all-start
  265.5 15.2 %scatter_custom_fusion.7 = f32[6,16384]{0,1:T(8,128)} fusion(s32[2048]{0:T(1024)S(1)} %bitcast.65, f32[2048,6]{1,0:T(8,128)S(1)} %copy.34, f32[]{:T(128)} %constant.21.clone.1..sunk), kind=kCustom, calls=%fused_computation.3.clone.1 | custom fusion | flops 12288 | bytes 393220 | tf_op jit(solution)/shard_map/while/body/eval_jaxpr/scatter-add | solution.py:55
  291.4 8.8 gather_fusion
  301.5 10.9 all-to-all-start
  328.3 15.2 %scatter_custom_fusion.7 = f32[6,16384]{0,1:T(8,128)} fusion(s32[2048]{0:T(1024)S(1)} %bitcast.65, f32[2048,6]{1,0:T(8,128)S(1)} %copy.34, f32[]{:T(128)} %constant.21.clone.1..sunk), kind=kCustom, calls=%fused_computation.3.clone.1 | custom fusion | flops 12288 | bytes 393220 | tf_op jit(solution)/shard_map/while/body/eval_jaxpr/scatter-add | solution.py:55
  364.2 10.9 all-to-all-start
  391.0 15.2 %scatter_custom_fusion.7 = f32[6,16384]{0,1:T(8,128)} fusion(s32[2048]{0:T(1024)S(1)} %bitcast.65, f32[2048,6]{1,0:T(8,128)S(1)} %copy.34, f32[]{:T(128)} %constant.21.clone.1..sunk), kind=kCustom, calls=%fused_computation.3.clone.1 | custom fusion | flops 12288 | bytes 393220 | tf_op jit(solution)/shard_map/while/body/eval_jaxpr/scatter-add | solution.py:55
  427.0 10.9 all-to-all-start
  453.7 15.2 %scatter_custom_fusion.7 = f32[6,16384]{0,1:T(8,128)} fusion(s32[2048]{0:T(1024)S(1)} %bitcast.65, f32[2048,6]{1,0:T(8,128)S(1)} %copy.34, f32[]{:T(128)} %constant.21.clone.1..sunk), kind=kCustom, calls=%fused_computation.3.clone.1 | custom fusion | flops 12288 | bytes 393220 | tf_op jit(solution)/shard_map/while/body/eval_jaxpr/scatter-add | solution.py:55
  479.6 8.8 gather_fusion
  489.7 10.9 all-to-all-start
  516.5 15.2 %scatter_custom_fusion.7 = f32[6,16384]{0,1:T(8,128)} fusion(s32[2048]{0:T(1024)S(1)} %bitcast.65, f32[2048,6]{1,0:T(8,128)S(1)} %copy.34, f32[]{:T(128)} %constant.21.clone.1..sunk), kind=kCustom, calls=%fused_computation.3.clone.1 | custom fusion | flops 12288 | bytes 393220 | tf_op jit(solution)/shard_map/while/body/eval_jaxpr/scatter-add | solution.py:55
  552.4 10.9 all-to-all-start
  579.2 15.2 %scatter_custom_fusion.7 = f32[6,16384]{0,1:T(8,128)} fusion(s32[2048]{0:T(1024)S(1)} %bitcast.65, f32[2048,6]{1,0:T(8,128)S(1)} %copy.34, f32[]{:T(128)} %constant.21.clone.1..sunk), kind=kCustom, calls=%fused_computation.3.clone.1 | custom fusion | flops 12288 | bytes 393220 | tf_op jit(solution)/shard_map/while/body/eval_jaxpr/scatter-add | solution.py:55
  605.1 8.8 gather_fusion
  615.2 10.9 all-to-all-start
  642.0 15.2 %scatter_custom_fusion.7 = f32[6,16384]{0,1:T(8,128)} fusion(s32[2048]{0:T(1024)S(1)} %bitcast.65, f32[2048,6]{1,0:T(8,128)S(1)} %copy.34, f32[]{:T(128)} %constant.21.clone.1..sunk), kind=kCustom, calls=%fused_computation.3.clone.1 | custom fusion | flops 12288 | bytes 393220 | tf_op jit(solution)/shard_map/while/body/eval_jaxpr/scatter-add | solution.py:55
  677.9 10.9 all-to-all-start
  704.7 15.2 %scatter_custom_fusion.7 = f32[6,16384]{0,1:T(8,128)} fusion(s32[2048]{0:T(1024)S(1)} %bitcast.65, f32[2048,6]{1,0:T(8,128)S(1)} %copy.34, f32[]{:T(128)} %constant.21.clone.1..sunk), kind=kCustom, calls=%fused_computation.3.clone.1 | custom fusion | flops 12288 | bytes 393220 | tf_op jit(solution)/shard_map/while/body/eval_jaxpr/scatter-add | solution.py:55
  740.6 10.9 all-to-all-start
  767.4 15.2 %scatter_custom_fusion.7 = f32[6,16384]{0,1:T(8,128)} fusion(s32[2048]{0:T(1024)S(1)} %bitcast.65, f32[2048,6]{1,0:T(8,128)S(1)} %copy.34, f32[]{:T(128)} %constant.21.clone.1..sunk), kind=kCustom, calls=%fused_computation.3.clone.1 | custom fusion | flops 12288 | bytes 393220 | tf_op jit(solution)/shard_map/while/body/eval_jaxpr/scatter-add | solution.py:55
  793.3 8.8 gather_fusion
  803.4 10.9 all-to-all-start
  830.2 15.2 %scatter_custom_fusion.7 = f32[6,16384]{0,1:T(8,128)} fusion(s32[2048]{0:T(1024)S(1)} %bitcast.65, f32[2048,6]{1,0:T(8,128)S(1)} %copy.34, f32[]{:T(128)} %constant.21.clone.1..sunk), kind=kCustom, calls=%fused_computation.3.clone.1 | custom fusion | flops 12288 | bytes 393220 | tf_op jit(solution)/shard_map/while/body/eval_jaxpr/scatter-add | solution.py:55
  866.1 10.9 all-to-all-start
  892.9 15.2 %scatter_custom_fusion.7 = f32[6,16384]{0,1:T(8,128)} fusion(s32[2048]{0:T(1024)S(1)} %bitcast.65, f32[2048,6]{1,0:T(8,128)S(1)} %copy.34, f32[]{:T(128)} %constant.21.clone.1..sunk), kind=kCustom, calls=%fused_computation.3.clone.1 | custom fusion | flops 12288 | bytes 393220 | tf_op jit(solution)/shard_map/while/body/eval_jaxpr/scatter-add | solution.py:55
  928.9 10.9 all-to-all-start
  955.7 15.2 %scatter_custom_fusion.7 = f32[6,16384]{0,1:T(8,128)} fusion(s32[2048]{0:T(1024)S(1)} %bitcast.65, f32[2048,6]{1,0:T(8,128)S(1)} %copy.34, f32[]{:T(128)} %constant.21.clone.1..sunk), kind=kCustom, calls=%fused_computation.3.clone.1 | custom fusion | flops 12288 | bytes 393220 | tf_op jit(solution)/shard_map/while/body/eval_jaxpr/scatter-add | solution.py:55
  981.5 8.8 gather_fusion
  991.6 10.9 all-to-all-start
  1018.4 15.2 %scatter_custom_fusion.7 = f32[6,16384]{0,1:T(8,128)} fusion(s32[2048]{0:T(1024)S(1)} %bitcast.65, f32[2048,6]{1,0:T(8,128)S(1)} %copy.34, f32[]{:T(128)} %constant.21.clone.1..sunk), kind=kCustom, calls=%fused_computation.3.clone.1 | custom fusion | flops 12288 | bytes 393220 | tf_op jit(solution)/shard_map/while/body/eval_jaxpr/scatter-add | solution.py:55
  1054.3 10.9 all-to-all-start
  1081.1 15.2 %scatter_custom_fusion.7 = f32[6,16384]{0,1:T(8,128)} fusion(s32[2048]{0:T(1024)S(1)} %bitcast.65, f32[2048,6]{1,0:T(8,128)S(1)} %copy.34, f32[]{:T(128)} %constant.21.clone.1..sunk), kind=kCustom, calls=%fused_computation.3.clone.1 | custom fusion | flops 12288 | bytes 393220 | tf_op jit(solution)/shard_map/while/body/eval_jaxpr/scatter-add | solution.py:55
  1117.1 10.9 all-to-all-start
  1143.9 15.2 %scatter_custom_fusion.7 = f32[6,16384]{0,1:T(8,128)} fusion(s32[2048]{0:T(1024)S(1)} %bitcast.65, f32[2048,6]{1,0:T(8,128)S(1)} %copy.34, f32[]{:T(128)} %constant.21.clone.1..sunk), kind=kCustom, calls=%fused_computation.3.clone.1 | custom fusion | flops 12288 | bytes 393220 | tf_op jit(solution)/shard_map/while/body/eval_jaxpr/scatter-add | solution.py:55
  1179.8 10.9 all-to-all-start
  1206.6 15.2 %scatter_custom_fusion.7 = f32[6,16384]{0,1:T(8,128)} fusion(s32[2048]{0:T(1024)S(1)} %bitcast.65, f32[2048,6]{1,0:T(8,128)S(1)} %copy.34, f32[]{:T(128)} %constant.21.clone.1..sunk), kind=kCustom, calls=%fused_computation.3.clone.1 | custom fusion | flops 12288 | bytes 393220 | tf_op jit(solution)/shard_map/while/body/eval_jaxpr/scatter-add | solution.py:55
  1242.6 10.9 all-to-all-start
  1269.3 15.2 %scatter_custom_fusion.7 = f32[6,16384]{0,1:T(8,128)} fusion(s32[2048]{0:T(1024)S(1)} %bitcast.65, f32[2048,6]{1,0:T(8,128)S(1)} %copy.34, f32[]{:T(128)} %constant.21.clone.1..sunk), kind=kCustom, calls=%fused_computation.3.clone.1 | custom fusion | flops 12288 | bytes 393220 | tf_op jit(solution)/shard_map/while/body/eval_jaxpr/scatter-add | solution.py:55
  (796 shorter events, 729.4 us)
Async XLA Ops:
  50.1 25.2 %all-to-all-start = ((f32[64,1,192]{2,1,0:T(1,128)}), f32[64,1,192]{2,1,0:T(1,128)S(1)}, u32[]{:S(2)}, u32[]{:S(2)}) async-start(f32[64,1,192]{2,1,0:T(1,128)} %reshape.136), calls=%async_computation | async-start | bytes 131072 | tf_op jit(solution)/shard_map/while/body/eval_jaxpr/all_to_all | solution.py:54
  68.8 29.1 %collective-permute-start.2 = (f32[6,66,1]{2,1,0:T(8,128)S(1)}, f32[6,66,1]{2,1,0:T(8,128)S(1)}, u32[]{:S(2)}, u32[]{:S(2)}) collective-permute-start(f32[6,66,1]{2,1,0:T(8,128)S(1)} %get-tuple-element.180), channel_id=1, source_target_pairs={{0,1},{1,2},{2,3},{3,4},{4,5},{5,6},{6,7},{8,9},{9,10},{10,11},{11... | collective-permute-start | bytes 4760 | tf_op jit(solution)/shard_map/while/body/eval_jaxpr/ppermute | solution.py:28
  73.4 24.5 %collective-permute-start.3 = (f32[6,66,1]{2,1,0:T(8,128)S(1)}, f32[6,66,1]{2,1,0:T(8,128)S(1)}, u32[]{:S(2)}, u32[]{:S(2)}) collective-permute-start(f32[6,66,1]{2,1,0:T(8,128)S(1)} %get-tuple-element.181), channel_id=1, source_target_pairs={{1,0},{2,1},{3,2},{4,3},{5,4},{6,5},{7,6},{9,8},{10,9},{11,10},{12... | collective-permute-start | bytes 4760 | tf_op jit(solution)/shard_map/while/body/eval_jaxpr/ppermute | solution.py:29
  113.3 24.8 %all-to-all-start = ((f32[64,1,192]{2,1,0:T(1,128)}), f32[64,1,192]{2,1,0:T(1,128)S(1)}, u32[]{:S(2)}, u32[]{:S(2)}) async-start(f32[64,1,192]{2,1,0:T(1,128)} %reshape.136), calls=%async_computation | async-start | bytes 131072 | tf_op jit(solution)/shard_map/while/body/eval_jaxpr/all_to_all | solution.py:54
  131.5 29.1 %collective-permute-start.2 = (f32[6,66,1]{2,1,0:T(8,128)S(1)}, f32[6,66,1]{2,1,0:T(8,128)S(1)}, u32[]{:S(2)}, u32[]{:S(2)}) collective-permute-start(f32[6,66,1]{2,1,0:T(8,128)S(1)} %get-tuple-element.180), channel_id=1, source_target_pairs={{0,1},{1,2},{2,3},{3,4},{4,5},{5,6},{6,7},{8,9},{9,10},{10,11},{11... | collective-permute-start | bytes 4760 | tf_op jit(solution)/shard_map/while/body/eval_jaxpr/ppermute | solution.py:28
  176.0 24.8 %all-to-all-start = ((f32[64,1,192]{2,1,0:T(1,128)}), f32[64,1,192]{2,1,0:T(1,128)S(1)}, u32[]{:S(2)}, u32[]{:S(2)}) async-start(f32[64,1,192]{2,1,0:T(1,128)} %reshape.136), calls=%async_computation | async-start | bytes 131072 | tf_op jit(solution)/shard_map/while/body/eval_jaxpr/all_to_all | solution.py:54
  194.2 29.1 %collective-permute-start.2 = (f32[6,66,1]{2,1,0:T(8,128)S(1)}, f32[6,66,1]{2,1,0:T(8,128)S(1)}, u32[]{:S(2)}, u32[]{:S(2)}) collective-permute-start(f32[6,66,1]{2,1,0:T(8,128)S(1)} %get-tuple-element.180), channel_id=1, source_target_pairs={{0,1},{1,2},{2,3},{3,4},{4,5},{5,6},{6,7},{8,9},{9,10},{10,11},{11... | collective-permute-start | bytes 4760 | tf_op jit(solution)/shard_map/while/body/eval_jaxpr/ppermute | solution.py:28
  198.8 24.5 %collective-permute-start.3 = (f32[6,66,1]{2,1,0:T(8,128)S(1)}, f32[6,66,1]{2,1,0:T(8,128)S(1)}, u32[]{:S(2)}, u32[]{:S(2)}) collective-permute-start(f32[6,66,1]{2,1,0:T(8,128)S(1)} %get-tuple-element.181), channel_id=1, source_target_pairs={{1,0},{2,1},{3,2},{4,3},{5,4},{6,5},{7,6},{9,8},{10,9},{11,10},{12... | collective-permute-start | bytes 4760 | tf_op jit(solution)/shard_map/while/body/eval_jaxpr/ppermute | solution.py:29
  238.7 24.8 %all-to-all-start = ((f32[64,1,192]{2,1,0:T(1,128)}), f32[64,1,192]{2,1,0:T(1,128)S(1)}, u32[]{:S(2)}, u32[]{:S(2)}) async-start(f32[64,1,192]{2,1,0:T(1,128)} %reshape.136), calls=%async_computation | async-start | bytes 131072 | tf_op jit(solution)/shard_map/while/body/eval_jaxpr/all_to_all | solution.py:54
  257.0 29.1 %collective-permute-start.2 = (f32[6,66,1]{2,1,0:T(8,128)S(1)}, f32[6,66,1]{2,1,0:T(8,128)S(1)}, u32[]{:S(2)}, u32[]{:S(2)}) collective-permute-start(f32[6,66,1]{2,1,0:T(8,128)S(1)} %get-tuple-element.180), channel_id=1, source_target_pairs={{0,1},{1,2},{2,3},{3,4},{4,5},{5,6},{6,7},{8,9},{9,10},{10,11},{11... | collective-permute-start | bytes 4760 | tf_op jit(solution)/shard_map/while/body/eval_jaxpr/ppermute | solution.py:28
  261.6 24.5 %collective-permute-start.3 = (f32[6,66,1]{2,1,0:T(8,128)S(1)}, f32[6,66,1]{2,1,0:T(8,128)S(1)}, u32[]{:S(2)}, u32[]{:S(2)}) collective-permute-start(f32[6,66,1]{2,1,0:T(8,128)S(1)} %get-tuple-element.181), channel_id=1, source_target_pairs={{1,0},{2,1},{3,2},{4,3},{5,4},{6,5},{7,6},{9,8},{10,9},{11,10},{12... | collective-permute-start | bytes 4760 | tf_op jit(solution)/shard_map/while/body/eval_jaxpr/ppermute | solution.py:29
  301.5 24.8 %all-to-all-start = ((f32[64,1,192]{2,1,0:T(1,128)}), f32[64,1,192]{2,1,0:T(1,128)S(1)}, u32[]{:S(2)}, u32[]{:S(2)}) async-start(f32[64,1,192]{2,1,0:T(1,128)} %reshape.136), calls=%async_computation | async-start | bytes 131072 | tf_op jit(solution)/shard_map/while/body/eval_jaxpr/all_to_all | solution.py:54
  319.7 29.1 %collective-permute-start.2 = (f32[6,66,1]{2,1,0:T(8,128)S(1)}, f32[6,66,1]{2,1,0:T(8,128)S(1)}, u32[]{:S(2)}, u32[]{:S(2)}) collective-permute-start(f32[6,66,1]{2,1,0:T(8,128)S(1)} %get-tuple-element.180), channel_id=1, source_target_pairs={{0,1},{1,2},{2,3},{3,4},{4,5},{5,6},{6,7},{8,9},{9,10},{10,11},{11... | collective-permute-start | bytes 4760 | tf_op jit(solution)/shard_map/while/body/eval_jaxpr/ppermute | solution.py:28
  364.2 24.8 %all-to-all-start = ((f32[64,1,192]{2,1,0:T(1,128)}), f32[64,1,192]{2,1,0:T(1,128)S(1)}, u32[]{:S(2)}, u32[]{:S(2)}) async-start(f32[64,1,192]{2,1,0:T(1,128)} %reshape.136), calls=%async_computation | async-start | bytes 131072 | tf_op jit(solution)/shard_map/while/body/eval_jaxpr/all_to_all | solution.py:54
  382.5 29.1 %collective-permute-start.2 = (f32[6,66,1]{2,1,0:T(8,128)S(1)}, f32[6,66,1]{2,1,0:T(8,128)S(1)}, u32[]{:S(2)}, u32[]{:S(2)}) collective-permute-start(f32[6,66,1]{2,1,0:T(8,128)S(1)} %get-tuple-element.180), channel_id=1, source_target_pairs={{0,1},{1,2},{2,3},{3,4},{4,5},{5,6},{6,7},{8,9},{9,10},{10,11},{11... | collective-permute-start | bytes 4760 | tf_op jit(solution)/shard_map/while/body/eval_jaxpr/ppermute | solution.py:28
  387.1 24.5 %collective-permute-start.3 = (f32[6,66,1]{2,1,0:T(8,128)S(1)}, f32[6,66,1]{2,1,0:T(8,128)S(1)}, u32[]{:S(2)}, u32[]{:S(2)}) collective-permute-start(f32[6,66,1]{2,1,0:T(8,128)S(1)} %get-tuple-element.181), channel_id=1, source_target_pairs={{1,0},{2,1},{3,2},{4,3},{5,4},{6,5},{7,6},{9,8},{10,9},{11,10},{12... | collective-permute-start | bytes 4760 | tf_op jit(solution)/shard_map/while/body/eval_jaxpr/ppermute | solution.py:29
  427.0 24.8 %all-to-all-start = ((f32[64,1,192]{2,1,0:T(1,128)}), f32[64,1,192]{2,1,0:T(1,128)S(1)}, u32[]{:S(2)}, u32[]{:S(2)}) async-start(f32[64,1,192]{2,1,0:T(1,128)} %reshape.136), calls=%async_computation | async-start | bytes 131072 | tf_op jit(solution)/shard_map/while/body/eval_jaxpr/all_to_all | solution.py:54
  445.2 29.1 %collective-permute-start.2 = (f32[6,66,1]{2,1,0:T(8,128)S(1)}, f32[6,66,1]{2,1,0:T(8,128)S(1)}, u32[]{:S(2)}, u32[]{:S(2)}) collective-permute-start(f32[6,66,1]{2,1,0:T(8,128)S(1)} %get-tuple-element.180), channel_id=1, source_target_pairs={{0,1},{1,2},{2,3},{3,4},{4,5},{5,6},{6,7},{8,9},{9,10},{10,11},{11... | collective-permute-start | bytes 4760 | tf_op jit(solution)/shard_map/while/body/eval_jaxpr/ppermute | solution.py:28
  449.8 24.5 %collective-permute-start.3 = (f32[6,66,1]{2,1,0:T(8,128)S(1)}, f32[6,66,1]{2,1,0:T(8,128)S(1)}, u32[]{:S(2)}, u32[]{:S(2)}) collective-permute-start(f32[6,66,1]{2,1,0:T(8,128)S(1)} %get-tuple-element.181), channel_id=1, source_target_pairs={{1,0},{2,1},{3,2},{4,3},{5,4},{6,5},{7,6},{9,8},{10,9},{11,10},{12... | collective-permute-start | bytes 4760 | tf_op jit(solution)/shard_map/while/body/eval_jaxpr/ppermute | solution.py:29
  489.7 24.8 %all-to-all-start = ((f32[64,1,192]{2,1,0:T(1,128)}), f32[64,1,192]{2,1,0:T(1,128)S(1)}, u32[]{:S(2)}, u32[]{:S(2)}) async-start(f32[64,1,192]{2,1,0:T(1,128)} %reshape.136), calls=%async_computation | async-start | bytes 131072 | tf_op jit(solution)/shard_map/while/body/eval_jaxpr/all_to_all | solution.py:54
  507.9 29.1 %collective-permute-start.2 = (f32[6,66,1]{2,1,0:T(8,128)S(1)}, f32[6,66,1]{2,1,0:T(8,128)S(1)}, u32[]{:S(2)}, u32[]{:S(2)}) collective-permute-start(f32[6,66,1]{2,1,0:T(8,128)S(1)} %get-tuple-element.180), channel_id=1, source_target_pairs={{0,1},{1,2},{2,3},{3,4},{4,5},{5,6},{6,7},{8,9},{9,10},{10,11},{11... | collective-permute-start | bytes 4760 | tf_op jit(solution)/shard_map/while/body/eval_jaxpr/ppermute | solution.py:28
  552.4 24.8 %all-to-all-start = ((f32[64,1,192]{2,1,0:T(1,128)}), f32[64,1,192]{2,1,0:T(1,128)S(1)}, u32[]{:S(2)}, u32[]{:S(2)}) async-start(f32[64,1,192]{2,1,0:T(1,128)} %reshape.136), calls=%async_computation | async-start | bytes 131072 | tf_op jit(solution)/shard_map/while/body/eval_jaxpr/all_to_all | solution.py:54
  570.7 29.1 %collective-permute-start.2 = (f32[6,66,1]{2,1,0:T(8,128)S(1)}, f32[6,66,1]{2,1,0:T(8,128)S(1)}, u32[]{:S(2)}, u32[]{:S(2)}) collective-permute-start(f32[6,66,1]{2,1,0:T(8,128)S(1)} %get-tuple-element.180), channel_id=1, source_target_pairs={{0,1},{1,2},{2,3},{3,4},{4,5},{5,6},{6,7},{8,9},{9,10},{10,11},{11... | collective-permute-start | bytes 4760 | tf_op jit(solution)/shard_map/while/body/eval_jaxpr/ppermute | solution.py:28
  575.3 24.5 %collective-permute-start.3 = (f32[6,66,1]{2,1,0:T(8,128)S(1)}, f32[6,66,1]{2,1,0:T(8,128)S(1)}, u32[]{:S(2)}, u32[]{:S(2)}) collective-permute-start(f32[6,66,1]{2,1,0:T(8,128)S(1)} %get-tuple-element.181), channel_id=1, source_target_pairs={{1,0},{2,1},{3,2},{4,3},{5,4},{6,5},{7,6},{9,8},{10,9},{11,10},{12... | collective-permute-start | bytes 4760 | tf_op jit(solution)/shard_map/while/body/eval_jaxpr/ppermute | solution.py:29
  615.2 24.8 %all-to-all-start = ((f32[64,1,192]{2,1,0:T(1,128)}), f32[64,1,192]{2,1,0:T(1,128)S(1)}, u32[]{:S(2)}, u32[]{:S(2)}) async-start(f32[64,1,192]{2,1,0:T(1,128)} %reshape.136), calls=%async_computation | async-start | bytes 131072 | tf_op jit(solution)/shard_map/while/body/eval_jaxpr/all_to_all | solution.py:54
  633.4 29.1 %collective-permute-start.2 = (f32[6,66,1]{2,1,0:T(8,128)S(1)}, f32[6,66,1]{2,1,0:T(8,128)S(1)}, u32[]{:S(2)}, u32[]{:S(2)}) collective-permute-start(f32[6,66,1]{2,1,0:T(8,128)S(1)} %get-tuple-element.180), channel_id=1, source_target_pairs={{0,1},{1,2},{2,3},{3,4},{4,5},{5,6},{6,7},{8,9},{9,10},{10,11},{11... | collective-permute-start | bytes 4760 | tf_op jit(solution)/shard_map/while/body/eval_jaxpr/ppermute | solution.py:28
  638.0 24.5 %collective-permute-start.3 = (f32[6,66,1]{2,1,0:T(8,128)S(1)}, f32[6,66,1]{2,1,0:T(8,128)S(1)}, u32[]{:S(2)}, u32[]{:S(2)}) collective-permute-start(f32[6,66,1]{2,1,0:T(8,128)S(1)} %get-tuple-element.181), channel_id=1, source_target_pairs={{1,0},{2,1},{3,2},{4,3},{5,4},{6,5},{7,6},{9,8},{10,9},{11,10},{12... | collective-permute-start | bytes 4760 | tf_op jit(solution)/shard_map/while/body/eval_jaxpr/ppermute | solution.py:29
  677.9 24.8 %all-to-all-start = ((f32[64,1,192]{2,1,0:T(1,128)}), f32[64,1,192]{2,1,0:T(1,128)S(1)}, u32[]{:S(2)}, u32[]{:S(2)}) async-start(f32[64,1,192]{2,1,0:T(1,128)} %reshape.136), calls=%async_computation | async-start | bytes 131072 | tf_op jit(solution)/shard_map/while/body/eval_jaxpr/all_to_all | solution.py:54
  696.2 29.1 %collective-permute-start.2 = (f32[6,66,1]{2,1,0:T(8,128)S(1)}, f32[6,66,1]{2,1,0:T(8,128)S(1)}, u32[]{:S(2)}, u32[]{:S(2)}) collective-permute-start(f32[6,66,1]{2,1,0:T(8,128)S(1)} %get-tuple-element.180), channel_id=1, source_target_pairs={{0,1},{1,2},{2,3},{3,4},{4,5},{5,6},{6,7},{8,9},{9,10},{10,11},{11... | collective-permute-start | bytes 4760 | tf_op jit(solution)/shard_map/while/body/eval_jaxpr/ppermute | solution.py:28
  700.7 24.5 %collective-permute-start.3 = (f32[6,66,1]{2,1,0:T(8,128)S(1)}, f32[6,66,1]{2,1,0:T(8,128)S(1)}, u32[]{:S(2)}, u32[]{:S(2)}) collective-permute-start(f32[6,66,1]{2,1,0:T(8,128)S(1)} %get-tuple-element.181), channel_id=1, source_target_pairs={{1,0},{2,1},{3,2},{4,3},{5,4},{6,5},{7,6},{9,8},{10,9},{11,10},{12... | collective-permute-start | bytes 4760 | tf_op jit(solution)/shard_map/while/body/eval_jaxpr/ppermute | solution.py:29
  740.6 24.8 %all-to-all-start = ((f32[64,1,192]{2,1,0:T(1,128)}), f32[64,1,192]{2,1,0:T(1,128)S(1)}, u32[]{:S(2)}, u32[]{:S(2)}) async-start(f32[64,1,192]{2,1,0:T(1,128)} %reshape.136), calls=%async_computation | async-start | bytes 131072 | tf_op jit(solution)/shard_map/while/body/eval_jaxpr/all_to_all | solution.py:54
  758.9 29.1 %collective-permute-start.2 = (f32[6,66,1]{2,1,0:T(8,128)S(1)}, f32[6,66,1]{2,1,0:T(8,128)S(1)}, u32[]{:S(2)}, u32[]{:S(2)}) collective-permute-start(f32[6,66,1]{2,1,0:T(8,128)S(1)} %get-tuple-element.180), channel_id=1, source_target_pairs={{0,1},{1,2},{2,3},{3,4},{4,5},{5,6},{6,7},{8,9},{9,10},{10,11},{11... | collective-permute-start | bytes 4760 | tf_op jit(solution)/shard_map/while/body/eval_jaxpr/ppermute | solution.py:28
  803.4 24.8 %all-to-all-start = ((f32[64,1,192]{2,1,0:T(1,128)}), f32[64,1,192]{2,1,0:T(1,128)S(1)}, u32[]{:S(2)}, u32[]{:S(2)}) async-start(f32[64,1,192]{2,1,0:T(1,128)} %reshape.136), calls=%async_computation | async-start | bytes 131072 | tf_op jit(solution)/shard_map/while/body/eval_jaxpr/all_to_all | solution.py:54
  821.6 29.1 %collective-permute-start.2 = (f32[6,66,1]{2,1,0:T(8,128)S(1)}, f32[6,66,1]{2,1,0:T(8,128)S(1)}, u32[]{:S(2)}, u32[]{:S(2)}) collective-permute-start(f32[6,66,1]{2,1,0:T(8,128)S(1)} %get-tuple-element.180), channel_id=1, source_target_pairs={{0,1},{1,2},{2,3},{3,4},{4,5},{5,6},{6,7},{8,9},{9,10},{10,11},{11... | collective-permute-start | bytes 4760 | tf_op jit(solution)/shard_map/while/body/eval_jaxpr/ppermute | solution.py:28
  866.1 24.8 %all-to-all-start = ((f32[64,1,192]{2,1,0:T(1,128)}), f32[64,1,192]{2,1,0:T(1,128)S(1)}, u32[]{:S(2)}, u32[]{:S(2)}) async-start(f32[64,1,192]{2,1,0:T(1,128)} %reshape.136), calls=%async_computation | async-start | bytes 131072 | tf_op jit(solution)/shard_map/while/body/eval_jaxpr/all_to_all | solution.py:54
  884.4 29.1 %collective-permute-start.2 = (f32[6,66,1]{2,1,0:T(8,128)S(1)}, f32[6,66,1]{2,1,0:T(8,128)S(1)}, u32[]{:S(2)}, u32[]{:S(2)}) collective-permute-start(f32[6,66,1]{2,1,0:T(8,128)S(1)} %get-tuple-element.180), channel_id=1, source_target_pairs={{0,1},{1,2},{2,3},{3,4},{4,5},{5,6},{6,7},{8,9},{9,10},{10,11},{11... | collective-permute-start | bytes 4760 | tf_op jit(solution)/shard_map/while/body/eval_jaxpr/ppermute | solution.py:28
  928.9 24.8 %all-to-all-start = ((f32[64,1,192]{2,1,0:T(1,128)}), f32[64,1,192]{2,1,0:T(1,128)S(1)}, u32[]{:S(2)}, u32[]{:S(2)}) async-start(f32[64,1,192]{2,1,0:T(1,128)} %reshape.136), calls=%async_computation | async-start | bytes 131072 | tf_op jit(solution)/shard_map/while/body/eval_jaxpr/all_to_all | solution.py:54
  947.1 29.1 %collective-permute-start.2 = (f32[6,66,1]{2,1,0:T(8,128)S(1)}, f32[6,66,1]{2,1,0:T(8,128)S(1)}, u32[]{:S(2)}, u32[]{:S(2)}) collective-permute-start(f32[6,66,1]{2,1,0:T(8,128)S(1)} %get-tuple-element.180), channel_id=1, source_target_pairs={{0,1},{1,2},{2,3},{3,4},{4,5},{5,6},{6,7},{8,9},{9,10},{10,11},{11... | collective-permute-start | bytes 4760 | tf_op jit(solution)/shard_map/while/body/eval_jaxpr/ppermute | solution.py:28
  991.6 24.8 %all-to-all-start = ((f32[64,1,192]{2,1,0:T(1,128)}), f32[64,1,192]{2,1,0:T(1,128)S(1)}, u32[]{:S(2)}, u32[]{:S(2)}) async-start(f32[64,1,192]{2,1,0:T(1,128)} %reshape.136), calls=%async_computation | async-start | bytes 131072 | tf_op jit(solution)/shard_map/while/body/eval_jaxpr/all_to_all | solution.py:54
  1009.9 29.1 %collective-permute-start.2 = (f32[6,66,1]{2,1,0:T(8,128)S(1)}, f32[6,66,1]{2,1,0:T(8,128)S(1)}, u32[]{:S(2)}, u32[]{:S(2)}) collective-permute-start(f32[6,66,1]{2,1,0:T(8,128)S(1)} %get-tuple-element.180), channel_id=1, source_target_pairs={{0,1},{1,2},{2,3},{3,4},{4,5},{5,6},{6,7},{8,9},{9,10},{10,11},{11... | collective-permute-start | bytes 4760 | tf_op jit(solution)/shard_map/while/body/eval_jaxpr/ppermute | solution.py:28
  1054.3 24.8 %all-to-all-start = ((f32[64,1,192]{2,1,0:T(1,128)}), f32[64,1,192]{2,1,0:T(1,128)S(1)}, u32[]{:S(2)}, u32[]{:S(2)}) async-start(f32[64,1,192]{2,1,0:T(1,128)} %reshape.136), calls=%async_computation | async-start | bytes 131072 | tf_op jit(solution)/shard_map/while/body/eval_jaxpr/all_to_all | solution.py:54
  1072.6 29.1 %collective-permute-start.2 = (f32[6,66,1]{2,1,0:T(8,128)S(1)}, f32[6,66,1]{2,1,0:T(8,128)S(1)}, u32[]{:S(2)}, u32[]{:S(2)}) collective-permute-start(f32[6,66,1]{2,1,0:T(8,128)S(1)} %get-tuple-element.180), channel_id=1, source_target_pairs={{0,1},{1,2},{2,3},{3,4},{4,5},{5,6},{6,7},{8,9},{9,10},{10,11},{11... | collective-permute-start | bytes 4760 | tf_op jit(solution)/shard_map/while/body/eval_jaxpr/ppermute | solution.py:28
  1117.1 24.8 %all-to-all-start = ((f32[64,1,192]{2,1,0:T(1,128)}), f32[64,1,192]{2,1,0:T(1,128)S(1)}, u32[]{:S(2)}, u32[]{:S(2)}) async-start(f32[64,1,192]{2,1,0:T(1,128)} %reshape.136), calls=%async_computation | async-start | bytes 131072 | tf_op jit(solution)/shard_map/while/body/eval_jaxpr/all_to_all | solution.py:54
  1135.3 29.1 %collective-permute-start.2 = (f32[6,66,1]{2,1,0:T(8,128)S(1)}, f32[6,66,1]{2,1,0:T(8,128)S(1)}, u32[]{:S(2)}, u32[]{:S(2)}) collective-permute-start(f32[6,66,1]{2,1,0:T(8,128)S(1)} %get-tuple-element.180), channel_id=1, source_target_pairs={{0,1},{1,2},{2,3},{3,4},{4,5},{5,6},{6,7},{8,9},{9,10},{10,11},{11... | collective-permute-start | bytes 4760 | tf_op jit(solution)/shard_map/while/body/eval_jaxpr/ppermute | solution.py:28
  1179.8 24.8 %all-to-all-start = ((f32[64,1,192]{2,1,0:T(1,128)}), f32[64,1,192]{2,1,0:T(1,128)S(1)}, u32[]{:S(2)}, u32[]{:S(2)}) async-start(f32[64,1,192]{2,1,0:T(1,128)} %reshape.136), calls=%async_computation | async-start | bytes 131072 | tf_op jit(solution)/shard_map/while/body/eval_jaxpr/all_to_all | solution.py:54
  1198.1 29.1 %collective-permute-start.2 = (f32[6,66,1]{2,1,0:T(8,128)S(1)}, f32[6,66,1]{2,1,0:T(8,128)S(1)}, u32[]{:S(2)}, u32[]{:S(2)}) collective-permute-start(f32[6,66,1]{2,1,0:T(8,128)S(1)} %get-tuple-element.180), channel_id=1, source_target_pairs={{0,1},{1,2},{2,3},{3,4},{4,5},{5,6},{6,7},{8,9},{9,10},{10,11},{11... | collective-permute-start | bytes 4760 | tf_op jit(solution)/shard_map/while/body/eval_jaxpr/ppermute | solution.py:28
  1242.6 24.8 %all-to-all-start = ((f32[64,1,192]{2,1,0:T(1,128)}), f32[64,1,192]{2,1,0:T(1,128)S(1)}, u32[]{:S(2)}, u32[]{:S(2)}) async-start(f32[64,1,192]{2,1,0:T(1,128)} %reshape.136), calls=%async_computation | async-start | bytes 131072 | tf_op jit(solution)/shard_map/while/body/eval_jaxpr/all_to_all | solution.py:54
  1260.8 29.1 %collective-permute-start.2 = (f32[6,66,1]{2,1,0:T(8,128)S(1)}, f32[6,66,1]{2,1,0:T(8,128)S(1)}, u32[]{:S(2)}, u32[]{:S(2)}) collective-permute-start(f32[6,66,1]{2,1,0:T(8,128)S(1)} %get-tuple-element.180), channel_id=1, source_target_pairs={{0,1},{1,2},{2,3},{3,4},{4,5},{5,6},{6,7},{8,9},{9,10},{10,11},{11... | collective-permute-start | bytes 4760 | tf_op jit(solution)/shard_map/while/body/eval_jaxpr/ppermute | solution.py:28
  (143 other events, 2537.6 us)
